TPU v7x, 128 devices: a whole 4x4x4 slice. The times are simulated.
128 devices in a mesh: wide: 16 (over y_lo, z, core), narrow: 8 (over x, y_hi).
Axes of the slice: x: 4, y: 4 (y_hi: 2, y_lo: 2; y = y_hi * 2 + y_lo), z: 4, core: 2. Of those that a mesh axis runs over, the one named last changes fastest.
Arguments:
- scalar_field: float32 [256, 512, 2048], P('wide', 'narrow'), may hold values from -6 to 6
- depth_rank: int32 [16], replicated, may hold values from 0 to 15, each once
- transfer: float32 [2, 3], replicated, may hold values from -2 to 2
- light_dir: float32 [3], replicated, may hold values from -1 to 1
Outputs:
- final_image: float32 [3, 512, 2048], P(None, 'narrow')
Inputs may be any that keep to these rules, and one draw needn't show every extreme that they name: `depth_rank`: every rank 0 to 15 appears exactly once.
All inputs are finite; a program needn't handle non-finite values.
Results may differ from a plain program's by a relative error of at most 0.000067.
Values sent between devices are 32-bit elements; how exact they have to be, the bound alone decides.
A program may use at most 128 MiB of HBM per device.

v0:
```python
import jax
import jax.numpy as jnp
from jax import lax
from jax.sharding import PartitionSpec as P

background = 0.25
optical_total = 2.0


def extended(value, sides, width):
    for axis, dim in sides:
        count, length = (lax.axis_size(axis), value.shape[dim])
        up = [(i, (i + 1) % count) for i in range(count - 1)]
        down = [(j, i) for i, j in up]
        last = lax.slice_in_dim(value, length - width, length, axis=dim)
        leading = lax.slice_in_dim(value, 0, width, axis=dim)
        before = lax.ppermute(last, axis, up)
        after = lax.ppermute(leading, axis, down)
        value = jnp.concatenate([before, value, after], axis=dim)
    return value


def march_steps(volume, plane_total):
    return jax.nn.softplus(2.0 * volume) * (optical_total / plane_total)


def render(padded, optical_step, light_dir, transfer):
    volume = padded[:, 1:-1, :]
    shifted_up = jnp.concatenate([volume[:1], volume[:-1]], axis=0)
    shifted_down = jnp.concatenate([volume[1:], volume[-1:]], axis=0)
    slope_depth = (shifted_down - shifted_up) * 0.5
    slope_rows = (padded[:, 2:, :] - padded[:, :-2, :]) * 0.5
    zero_column = jnp.zeros_like(volume[:, :, :1])
    right_cells = jnp.concatenate([volume[:, :, 1:], zero_column], axis=2)
    left_cells = jnp.concatenate([zero_column, volume[:, :, :-1]], axis=2)
    slope_cols = (right_cells - left_cells) * 0.5
    shading = 0.5 + 0.5 * jnp.tanh(
        light_dir[0] * slope_depth + light_dir[1] * slope_rows + light_dir[2] * slope_cols
    )
    passed = jnp.cumsum(optical_step, axis=0) - optical_step
    weights = jnp.exp(-passed) * (1.0 - jnp.exp(-optical_step)) * shading
    colors = jax.nn.sigmoid(
        transfer[0][:, None, None, None] * volume[None] + transfer[1][:, None, None, None]
    )
    return jnp.sum(weights[None] * colors, axis=1)


def body(scalar_field, depth_rank, transfer, light_dir):
    plane_count = scalar_field.shape[0]
    wide_count = lax.axis_size("wide")
    columns = scalar_field.shape[2]
    col_block = columns // wide_count
    wide_index = lax.axis_index("wide")
    optical_step = march_steps(scalar_field, plane_count * wide_count)
    brick_depth = jnp.sum(optical_step, axis=0)
    padded = extended(scalar_field, (("narrow", 1),), 1)
    shaded_color = render(padded, optical_step, light_dir, transfer)
    my_rank = lax.dynamic_index_in_dim(depth_rank, wide_index, keepdims=False)
    pieces = lax.all_gather(brick_depth[None], "wide", axis=0, tiled=True)
    in_front = (depth_rank < my_rank).astype(jnp.float32)
    ahead = jnp.einsum("k,kyx->yx", in_front, pieces, precision=lax.Precision.HIGHEST)
    total_depth = jnp.sum(pieces, axis=0)
    weighted = jnp.exp(-ahead)[None] * shaded_color
    partial_value = lax.psum_scatter(weighted, "wide", scatter_dimension=2, tiled=True)
    total_cols = lax.dynamic_slice_in_dim(total_depth, wide_index * col_block, col_block, 1)
    image_tile = partial_value + background * jnp.exp(-total_cols)
    return lax.all_gather(image_tile, "wide", axis=2, tiled=True)


def solution(mesh):
    return jax.shard_map(
        body,
        mesh=mesh,
        in_specs=(P("wide", "narrow", None), P(), P(), P()),
        out_specs=P(None, "narrow", None),
        check_vma=False,
    )
```

profile of v0, /device:TPU:1, one launch (start us, length us, event | category | flops | bytes accessed | tf_op | source)
XLA Modules:
  0.0 255.3 jit_solution(6576075107872943503)
XLA Ops:
  6.5 1.7 fusion.25
  8.3 1.3 collective-permute-start
  9.6 6.3 %collective-permute-start.1 = (f32[16,1,2048]{2,1,0:T(1,128)S(1)}, f32[16,1,2048]{2,1,0:T(1,128)S(1)}, u32[]{:S(2)}, u32[]{:S(2)}) collective-permute-start(f32[16,1,2048]{2,1,0:T(1,128)S(1)} %get-tuple-element.14), channel_id=1, source_target_pairs={{0,1},{1,2},{2,3},{3,4},{4,5},{5,6},{6,7},{8,9},{9,10},{10,11},{11... | collective-permute-start | bytes 393224 | tf_op jit(solution)/shard_map/ppermute | solution.py:17
  15.9 13.2 %fusion.22 = (f32[16,64,2047]{2,1,0:T(8,128)}, f32[16,64,2047]{2,1,0:T(8,128)}) fusion(f32[16,64,2048]{2,1,0:T(8,128)} %param.4), kind=kLoop, calls=%fused_computation.32 | loop fusion | bytes 33538048 | tf_op jit(solution)/shard_map/slice | solution.py:34
  29.1 13.9 %fusion.24 = (f32[15,64,2048]{2,1,0:T(8,128)}, f32[15,64,2048]{2,1,0:T(8,128)}) fusion(f32[16,64,2048]{2,1,0:T(8,128)} %param.4), kind=kLoop, calls=%fused_computation.34 | loop fusion | bytes 31457280 | tf_op jit(solution)/shard_map/slice | solution.py:29
  43.0 1.3 fusion.23
  44.3 0.7 fusion.26
  46.9 29.9 %fusion.14 = (f32[64,2048]{1,0:T(8,128)}, f32[16,64,2048]{2,1,0:T(8,128)}) fusion(f32[16,64,2048]{2,1,0:T(8,128)} %param.4, f32[]{:T(128)} %bitcast.6, f32[16,64,2047]{2,1,0:T(8,128)} %get-tuple-element.8, f32[16,64,2047]{2,1,0:T(8,128)} %get-tuple-element.7, f32[]{:T(128)} %bitcast.5, f32[16,1,2048]{2,1,0:T(1,128)S(1)} %collective-permute-done.1, ...), kind=kOutput, calls=%fused_computation.18 | output fusion | flops 108920832 | bytes 51109900 | tf_op jit(solution)/shard_map/jit(cumsum)/reduce_window_sum | solution.py:40
  76.8 0.0 all-gather.6.cloned.1.call-update
  76.8 0.2 reduce-scatter.2.cloned.1.call-start
  77.1 0.6 dynamic_slice.7
  77.7 9.0 %multiply_reduce_fusion = f32[3,64,2048]{2,1,0:T(8,128)S(1)} fusion(f32[3]{0:T(128)S(1)} %get-tuple-element.16, f32[16,64,2048]{2,1,0:T(8,128)} %param.4, f32[3]{0:T(128)S(1)} %get-tuple-element.15, f32[16,64,2048]{2,1,0:T(8,128)} %get-tuple-element.6), kind=kLoop, calls=%fused_computation | loop fusion | flops 43646976 | bytes 18350104 | tf_op jit(solution)/shard_map/reduce_sum | solution.py:45
  86.7 46.8 %all-gather.6.cloned.1.call-done = f32[1024,2048]{1,0:T(8,128)} async-done(((f32[64,2048]{1,0:T(8,128)}), f32[1024,2048]{1,0:T(8,128)}) %all-gather.6.cloned.1.call-update) | async-done | bytes 8388624 | tf_op jit(solution)/shard_map/all_gather | solution.py:59
  133.5 11.3 %fusion.10 = f32[1,64,2048]{2,0,1:T(1,128)S(1)} fusion(f32[16,64,2048]{2,1,0:T(8,128)} %bitcast.16, s32[16]{0:T(128)S(1)} %copy-done.2, s32[]{:T(128)} %bitcast), kind=kOutput, calls=%fused_computation.15 | convolution fusion | flops 25165840 | bytes 8912964 | tf_op jit(solution)/shard_map/k,kyx->yx/dot_general | solution.py:61
  144.8 0.2 fusion.15
  145.0 1.3 broadcast_multiply_fusion
  146.3 0.0 reduce-scatter.2.cloned.1.call-update
  146.3 0.0 all-gather.4.cloned.1.call-start
  146.4 3.9 %reduce_sum.29 = f32[64,2048]{1,0:T(8,128)S(1)} reduce(f32[16,64,2048]{2,1,0:T(8,128)} %bitcast.17, f32[]{:T(128)} %constant.18.clone.1), dimensions={0}, to_apply=%region_4.5 | reduce | flops 1966080 | bytes 8912900 | tf_op jit(solution)/shard_map/reduce_sum | solution.py:62
  150.4 55.3 %reduce-scatter.2.cloned.1.call-done = f32[3,64,128]{2,1,0:T(8,128)} async-done(((f32[3,64,2048]{2,1,0:T(8,128)}), f32[3,64,128]{2,1,0:T(8,128)}) %reduce-scatter.2.cloned.1.call-update) | async-done | bytes 98320 | tf_op jit(solution)/shard_map/reduce_scatter | solution.py:64
  205.7 1.5 broadcast_add_fusion
  207.2 0.0 all-gather.4.cloned.1.call-update
  207.3 38.8 %all-gather.4.cloned.1.call-done = f32[3,64,2048]{2,1,0:T(8,128)} async-done(((f32[3,64,128]{2,1,0:T(8,128)}), f32[3,64,2048]{2,1,0:T(8,128)}) %all-gather.4.cloned.1.call-update) | async-done | bytes 1572880 | tf_op jit(solution)/shard_map/all_gather | solution.py:67
  246.0 2.7 %copy.11 = f32[3,64,2048]{2,1,0:T(8,128)} copy(f32[3,64,2048]{2,1,0:T(8,128)} %all-gather.4.cloned.1.call-done) | data formatting | bytes 3145728
  (11 shorter events, 0.0 us)
Async XLA Ops:
  6.5 126.9 %all-gather.6.cloned.1.call-start = ((), (), s32[]{:S(2)}) async-start(), calls=%async_computation.3 | async-start | bytes 8912896 | tf_op jit(solution)/shard_map/all_gather | solution.py:59
  8.3 38.6 %collective-permute-start = (f32[16,1,2048]{2,1,0:T(1,128)S(1)}, f32[16,1,2048]{2,1,0:T(1,128)S(1)}, u32[]{:S(2)}, u32[]{:S(2)}) collective-permute-start(f32[16,1,2048]{2,1,0:T(1,128)S(1)} %get-tuple-element.13), channel_id=1, source_target_pairs={{1,0},{2,1},{3,2},{4,3},{5,4},{6,5},{7,6},{9,8},{10,9},{11,10},{12... | collective-permute-start | bytes 393224 | tf_op jit(solution)/shard_map/ppermute | solution.py:18
  9.6 37.3 %collective-permute-start.1 = (f32[16,1,2048]{2,1,0:T(1,128)S(1)}, f32[16,1,2048]{2,1,0:T(1,128)S(1)}, u32[]{:S(2)}, u32[]{:S(2)}) collective-permute-start(f32[16,1,2048]{2,1,0:T(1,128)S(1)} %get-tuple-element.14), channel_id=1, source_target_pairs={{0,1},{1,2},{2,3},{3,4},{4,5},{5,6},{6,7},{8,9},{9,10},{10,11},{11... | collective-permute-start | bytes 393224 | tf_op jit(solution)/shard_map/ppermute | solution.py:17
  29.1 15.2 %copy-start = (f32[3]{0:T(128)S(1)}, f32[3]{0:T(128)}, u32[]{:S(2)}) copy-start(f32[3]{0:T(128)} %param.7) | copy-start | bytes 40
  46.9 30.2 %copy-start.2 = (s32[16]{0:T(128)S(1)}, s32[16]{0:T(128)}, u32[]{:S(2)}) copy-start(s32[16]{0:T(128)} %param.5) | copy-start | bytes 196
  46.9 30.8 %copy-start.1 = (f32[2,3]{1,0:T(2,128)S(1)}, f32[2,3]{1,0:T(2,128)}, u32[]{:S(2)}) copy-start(f32[2,3]{1,0:T(2,128)} %param.6) | copy-start | bytes 76
  76.8 128.8 %reduce-scatter.2.cloned.1.call-start = ((), (), s32[]{:S(2)}) async-start(), calls=%async_computation.1 | async-start | bytes 1671168 | tf_op jit(solution)/shard_map/reduce_scatter | solution.py:64
  146.3 99.7 %all-gather.4.cloned.1.call-start = ((), (), s32[]{:S(2)}) async-start(), calls=%async_computation.2 | async-start | bytes 1671168 | tf_op jit(solution)/shard_map/all_gather | solution.py:67
Sparse Core Ops, SparseCore 0:
  77.0 56.4 all-gather.5
  146.4 59.1 reduce-scatter.1
  207.4 38.5 all-gather.3
where the time goes:
time: 256 us; the launch traced here: 255 us
  waiting for transfers between devices  141 us (55%)
  other arithmetic  45.9 us (18%)
  local copies, waits for them, and re-layouts  34.1 us (13%)
  between operations  15.1 us (6%)
  matrix products  11.3 us (4%)
  starting transfers between devices  7.84 us (3%)
    reduce_scatter x1, waiting for transfers between devices, body(): lax.psum_scatter(weighted, 'wide', scatter_dimension=2, tiled=True)  55.3 us
    all_gather x1, waiting for transfers between devices, body(): pieces = lax.all_gather(brick_depth[None], 'wide', axis=0, tiled=True)  46.8 us
    all_gather x1, waiting for transfers between devices, body(): return lax.all_gather(image_tile, 'wide', axis=2, tiled=True)  38.8 us
    another operation x1, other arithmetic, render(): passed = jnp.cumsum(optical_step, axis=0) - optical_step  29.9 us
    slice x2, local copies, waits for them, and re-layouts, render(): shifted_up = jnp.concatenate([volume[:1], volume[:-1]], axis=0)  15.2 us
    slice x1, local copies, waits for them, and re-layouts, render(): right_cells = jnp.concatenate([volume[:, :, 1:], zero_column], axis=2)  13.2 us
    dot_general x1, matrix products, body(): jnp.einsum('k,kyx->yx', in_front, pieces, precision=lax.Precision.HIGHEST)  11.3 us
    reduce_sum x1, other arithmetic, render(): return jnp.sum(weights[None] * colors, axis=1)  8.96 us
  transfers between devices with their start and end apart: 5, of which 3 were waited for; matrix products, arithmetic and copies ran while one was open for 17% of the time, Pallas kernels for 0%

commit v1 on v0

v1 whole, which is shorter than its diff:
```python
import functools
import math

import jax
import jax.numpy as jnp
from jax import lax
from jax.experimental import pallas as pl
from jax.experimental.pallas import tpu as pltpu
from jax.sharding import PartitionSpec as P

MESH = pl.DeviceIdType.MESH
BACKGROUND = 0.25
LOG2E = math.log2(math.e)
LAG = 2
PARTNERS = (
    (1, 2, 0), (1, 0, 0), (0, 2, 0), (0, 1, 0), (1, 1, 0), (0, 3, 0), (1, 3, 0),
    (1, 2, 1), (1, 0, 1), (0, 2, 1), (0, 1, 1), (1, 1, 1), (0, 3, 1), (1, 3, 1),
    (0, 0, 1),
)


def brick_cells(vol, tile, row, scale, light, trans):
    planes = vol.shape[0]
    lane = lax.broadcasted_iota(jnp.int32, (8, 128), 1)
    first, last = lane == 0, lane == 127
    zero = jnp.zeros((8, 128), jnp.float32)
    depth, through = zero, zero + 1.0
    acc = [zero] * 3
    value = vol[0, tile, pl.ds(row, 8), :]
    before = value
    for p in range(planes):
        after = vol[p + 1, tile, pl.ds(row, 8), :] if p + 1 < planes else value
        up = vol[p, tile, pl.ds(row - 1, 8), :]
        down = vol[p, tile, pl.ds(row + 1, 8), :]
        right = pltpu.roll(jnp.where(first, vol[p, tile + 1, pl.ds(row, 8), :], value), 127, 1)
        left = pltpu.roll(jnp.where(last, vol[p, tile - 1, pl.ds(row, 8), :], value), 1, 1)
        slope = light[0] * (after - before) + light[1] * (down - up) + light[2] * (right - left)
        depth = depth + jnp.log(1.0 + jnp.exp2(value * (2.0 * LOG2E)))
        beyond = jnp.exp2(depth * (-scale * LOG2E))
        weight = through - beyond
        through = beyond
        shaded = weight + weight * jnp.tanh(slope)
        den = [1.0 + jnp.exp2(trans[0][c] * value + trans[1][c]) for c in range(3)]
        den01 = den[0] * den[1]
        part = shaded / (den01 * den[2])
        part2 = part * den[2]
        acc[0] = acc[0] + part2 * den[1]
        acc[1] = acc[1] + part2 * den[0]
        acc[2] = acc[2] + part * den01
        before, value = value, after
    return acc, depth


def kernel(
    sizes, field, rank, transfer, light_dir, out,
    vol, send, recv, image, front,
    load_sem, halo_ssem, halo_rsem, send_sem, recv_sem, ag_ssem, ag_rsem, out_sem,
):
    wide, narrow, rows, scale = sizes
    blocks = wide
    chunks = rows // 8
    me = lax.axis_index("wide")
    row_part = lax.axis_index("narrow")
    y, z, core = me // 8, (me // 2) % 4, me % 2

    def device(dy, dz, dc):
        return ((y + dy) % 2) * 8 + ((z + dz) % 4) * 2 + (core + dc) % 2

    def column_block(dy, dz, dc):
        return ((core + dc) % 2) * 8 + ((z + dz) % 4) * 2 + (y + dy) % 2

    mine = column_block(0, 0, 0)

    barrier = pltpu.get_barrier_semaphore()
    for dy, dz, dc in PARTNERS:
        pl.semaphore_signal(barrier, inc=1, device_id=(device(dy, dz, dc), row_part), device_id_type=MESH)

    @pl.when(row_part > 0)
    def _():
        pl.semaphore_signal(barrier, inc=1, device_id=(me, row_part - 1), device_id_type=MESH)

    @pl.when(row_part < narrow - 1)
    def _():
        pl.semaphore_signal(barrier, inc=1, device_id=(me, row_part + 1), device_id_type=MESH)

    def load(k, part):
        lo, n = ((0, 24), (24, rows - 24))[part]
        return pltpu.make_async_copy(
            field.at[:, lo:lo + n, pl.ds(pl.multiple_of(k * 128, 128), 128)],
            vol.at[:, k + 1, 8 + lo:8 + lo + n, :],
            load_sem.at[part, k],
        )

    for part in range(2):
        def start_load(k, _, part=part):
            load(k, part).start()
            return 0
        lax.fori_loop(0, blocks, start_load, 0)

    def clear(p, _):
        vol[p, 0, 8:8 + rows, :] = jnp.zeros((rows, 128), jnp.float32)
        vol[p, blocks + 1, 8:8 + rows, :] = jnp.zeros((rows, 128), jnp.float32)
        return 0

    lax.fori_loop(0, vol.shape[0], clear, 0)

    def clear_row(at):
        def step(p, _):
            vol[p, 1:blocks + 1, at:at + 1, :] = jnp.zeros((blocks, 1, 128), jnp.float32)
            return 0
        lax.fori_loop(0, vol.shape[0], step, 0)

    @pl.when(row_part == 0)
    def _():
        clear_row(7)

    @pl.when(row_part == narrow - 1)
    def _():
        clear_row(8 + rows)

    for b in range(wide):
        for o in range(wide):
            front[b * wide + o] = jnp.where(rank[o] < rank[b], 1.0, 0.0)

    light = [0.5 * light_dir[i] for i in range(3)]
    trans = [[-LOG2E * transfer[i, c] for c in range(3)] for i in range(2)]

    def wait_load(part):
        lo, n = ((0, 24), (24, rows - 24))[part]
        for k in range(blocks):
            load(k, part).wait()

    def compute(chunk):
        row = 8 + 8 * chunk

        def step(k, _):
            acc, depth = brick_cells(vol, k + 1, row, scale, light, trans)
            for c in range(3):
                send[chunk, k, c] = acc[c] * 0.5
            send[chunk, k, 3] = depth * scale
            return 0

        lax.fori_loop(0, blocks, step, 0)

    def block_copy(chunk, dy, dz, dc):
        return pltpu.make_async_remote_copy(
            src_ref=send.at[chunk, column_block(dy, dz, dc)],
            dst_ref=recv.at[chunk, me],
            send_sem=send_sem.at[chunk],
            recv_sem=recv_sem.at[chunk],
            device_id=(device(dy, dz, dc), row_part),
            device_id_type=MESH,
        )

    def send_chunk(chunk):
        for partner in PARTNERS:
            block_copy(chunk, *partner).start()

    def all_of(chunk):
        part = recv.at[chunk, 0:wide - 1]
        return pltpu.make_async_remote_copy(
            src_ref=send.at[chunk, 0:wide - 1], dst_ref=part, send_sem=send_sem.at[chunk], recv_sem=recv_sem.at[chunk],
            device_id=(device(1, 0, 0), row_part), device_id_type=MESH,
        )

    def composite(chunk):
        recv[chunk, me] = send[chunk, mine]
        all_of(chunk).wait_recv()
        depths = [recv[chunk, b, 3] for b in range(wide)]
        total = depths[0]
        for b in range(1, wide):
            total = total + depths[b]
        back = BACKGROUND * jnp.exp(-total)
        acc = [back] * 3
        for b in range(wide):
            ahead = jnp.zeros((8, 128), jnp.float32)
            for o in range(wide):
                if o != b:
                    ahead = ahead + front[b * wide + o] * depths[o]
            seen = jnp.exp(-ahead)
            for c in range(3):
                acc[c] = acc[c] + seen * recv[chunk, b, c]
        for c in range(3):
            image[c, chunk * 8:chunk * 8 + 8, pl.ds(pl.multiple_of(mine * 128, 128), 128)] = acc[c]

    def tile(chunk, start, count):
        return image.at[:, chunk * 8:chunk * 8 + 8, pl.ds(pl.multiple_of(start * 128, 128), count * 128)]

    def gather_copy(chunk, slot, start, count, dy, dz, dc, got):
        def made(at):
            return pltpu.make_async_remote_copy(
                src_ref=tile(chunk, at, count), dst_ref=tile(chunk, at, count),
                send_sem=ag_ssem.at[chunk, slot], recv_sem=ag_rsem.at[chunk, slot],
                device_id=(device(dy, dz, dc), row_part), device_id_type=MESH,
            )
        return functools.partial(made, start), functools.partial(made, got)

    def pair(dz):
        return core * 8 + ((z + dz) % 4) * 2

    def stage1(chunk):
        return [gather_copy(chunk, 0, mine, 1, 1, 0, 0, column_block(1, 0, 0))]

    def stage2(chunk):
        return [
            gather_copy(chunk, 1, pair(0), 2, 0, 1, 0, pair(3)),
            gather_copy(chunk, 2, pair(0), 2, 0, 3, 0, pair(1)),
        ]

    def stage3(chunk):
        return [
            gather_copy(chunk, 3, pair(3), 1, 0, 1, 0, pair(2)),
            gather_copy(chunk, 4, pair(1) + 1, 1, 0, 3, 0, pair(2) + 1),
        ]

    def stage4(chunk):
        return [gather_copy(chunk, 5, core * 8, 8, 0, 0, 1, ((core + 1) % 2) * 8)]

    stages = (stage1, stage2, stage3, stage4)

    def begin(stage, chunk):
        for sent, _ in stages[stage](chunk):
            sent().start()

    def end(stage, chunk):
        for _, got in stages[stage](chunk):
            got().wait_recv()

    def write(chunk):
        return pltpu.make_async_copy(
            image.at[:, chunk * 8:chunk * 8 + 8, :], out.at[:, chunk * 8:chunk * 8 + 8, :], out_sem.at[chunk]
        )

    def halo_up():
        return pltpu.make_async_remote_copy(
            src_ref=vol.at[:, 1:blocks + 1, 8:9, :], dst_ref=vol.at[:, 1:blocks + 1, 8 + rows:9 + rows, :],
            send_sem=halo_ssem.at[0], recv_sem=halo_rsem.at[0],
            device_id=(me, row_part - 1), device_id_type=MESH,
        )

    def halo_down():
        return pltpu.make_async_remote_copy(
            src_ref=vol.at[:, 1:blocks + 1, 7 + rows:8 + rows, :], dst_ref=vol.at[:, 1:blocks + 1, 7:8, :],
            send_sem=halo_ssem.at[1], recv_sem=halo_rsem.at[1],
            device_id=(me, row_part + 1), device_id_type=MESH,
        )

    has_up, has_down = row_part > 0, row_part < narrow - 1
    order = list(range(1, chunks - 1)) + [0, chunks - 1]
    last = chunks + LAG + 4
    for step in range(last):
        if step == 0:
            wait_load(0)
        if step < chunks:
            chunk = order[step]
            if chunk == 0:
                @pl.when(has_up)
                def _():
                    halo_down().wait_recv()
            if chunk == chunks - 1:
                @pl.when(has_down)
                def _():
                    halo_up().wait_recv()
            compute(chunk)
        if step == 0:
            wait_load(1)
            pl.semaphore_wait(barrier, wide - 1 + has_up.astype(jnp.int32) + has_down.astype(jnp.int32))

            @pl.when(has_up)
            def _():
                halo_up().start()

            @pl.when(has_down)
            def _():
                halo_down().start()
        if step < chunks:
            send_chunk(order[step])
        for stage in range(4, -1, -1):
            at = step - LAG - stage
            if 0 <= at < chunks:
                chunk = order[at]
                if stage == 0:
                    composite(chunk)
                    begin(0, chunk)
                else:
                    end(stage - 1, chunk)
                    if stage < 4:
                        begin(stage, chunk)
                    else:
                        write(chunk).start()

    for chunk in range(chunks):
        all_of(chunk).wait_send()
        for stage in range(4):
            for sent, _ in stages[stage](chunk):
                sent().wait_send()
        write(chunk).wait()

    @pl.when(has_up)
    def _():
        halo_up().wait_send()

    @pl.when(has_down)
    def _():
        halo_down().wait_send()


def solution(mesh):
    wide, narrow = mesh.shape["wide"], mesh.shape["narrow"]

    def body(scalar_field, depth_rank, transfer, light_dir):
        planes, rows, columns = scalar_field.shape
        blocks = columns // 128
        chunks = rows // 8
        scale = 2.0 / (planes * wide)
        smem = pl.BlockSpec(memory_space=pltpu.SMEM)
        return pl.pallas_call(
            functools.partial(kernel, (wide, narrow, rows, scale)),
            out_shape=jax.ShapeDtypeStruct((3, rows, columns), jnp.float32),
            in_specs=[pl.BlockSpec(memory_space=pl.ANY), smem, smem, smem],
            out_specs=pl.BlockSpec(memory_space=pl.ANY),
            scratch_shapes=[
                pltpu.VMEM((planes, blocks + 2, rows + 16, 128), jnp.float32),
                pltpu.VMEM((chunks, blocks, 4, 8, 128), jnp.float32),
                pltpu.VMEM((chunks, wide, 4, 8, 128), jnp.float32),
                pltpu.VMEM((3, rows, columns), jnp.float32),
                pltpu.SMEM((wide * wide,), jnp.float32),
                pltpu.SemaphoreType.DMA((2, blocks)),
                pltpu.SemaphoreType.DMA((2,)),
                pltpu.SemaphoreType.DMA((2,)),
                pltpu.SemaphoreType.DMA((chunks,)),
                pltpu.SemaphoreType.DMA((chunks,)),
                pltpu.SemaphoreType.DMA((chunks, 6)),
                pltpu.SemaphoreType.DMA((chunks, 6)),
                pltpu.SemaphoreType.DMA((chunks,)),
            ],
            compiler_params=pltpu.CompilerParams(collective_id=0, has_side_effects=True),
        )(scalar_field, depth_rank, transfer, light_dir)

    return jax.shard_map(
        body,
        mesh=mesh,
        in_specs=(P("wide", "narrow", None), P(), P(), P()),
        out_specs=P(None, "narrow", None),
        check_vma=False,
    )
```

time: 256 us -> 67.5 us (0.26)
  waiting for transfers between devices: 141 us -> 0 us
  Pallas kernels: 0 us -> 64.7 us
  other arithmetic: 45.9 us -> 0 us
  local copies, waits for them, and re-layouts: 34.1 us -> 2.7 us
  between operations: 15.1 us -> 0.01 us
  matrix products: 11.3 us -> 0 us
  starting transfers between devices: 7.84 us -> 0 us
    all_gather x2 -> x0, waiting for transfers between devices: 85.6 us -> none  [the longest x1 46.8 us: body(): pieces = lax.all_gather(brick_depth[None], 'wide', axis=0, tiled=True)]
    pallas_call x0 -> x1, Pallas kernels: none -> 64.7 us  [body(): pl.pallas_call(functools.partial(kernel, (wide, narrow, rows, scale)), ou...]
    reduce_scatter x1 -> x0, waiting for transfers between devices: 55.3 us -> none  [body(): lax.psum_scatter(weighted, 'wide', scatter_dimension=2, tiled=True)]
    slice x5 -> x0, local copies, waits for them, and re-layouts: 30.8 us -> none  [the longest x2 15.2 us: render(): shifted_up = jnp.concatenate([volume[:1], volume[:-1]], axis=0)]
    another operation x1 -> x0, other arithmetic: 29.9 us -> none  [render(): passed = jnp.cumsum(optical_step, axis=0) - optical_step]
    reduce_sum x2 -> x0, other arithmetic: 12.9 us -> none  [the longest x1 8.96 us: render(): return jnp.sum(weights[None] * colors, axis=1)]
    dot_general x1 -> x0, matrix products: 11.3 us -> none  [body(): jnp.einsum('k,kyx->yx', in_front, pieces, precision=lax.Precision.HIGHEST)]
    ppermute x2 -> x0, starting transfers between devices: 7.58 us -> none  [the longest x1 6.28 us: extended(): before = lax.ppermute(last, axis, up)]
  transfers between devices with their start and end apart: 5 -> 0, of which waited for: 3 -> 0; matrix products, arithmetic and copies ran while one was open for 17% -> 0% of each run, Pallas kernels for 0% -> 0%
where the time goes in v1:
time: 67.5 us; the launch traced here: 67.4 us
  Pallas kernels  64.7 us (96%)
  local copies, waits for them, and re-layouts  2.7 us (4%)
    pallas_call x1, Pallas kernels, body(): pl.pallas_call(functools.partial(kernel, (wide, narrow, rows, scale)), ou...  64.7 us
    unnamed x1, local copies, waits for them, and re-layouts  2.7 us

profile of v1, /device:TPU:1, one launch (start us, length us, event | category | flops | bytes accessed | tf_op | source)
XLA Modules:
  0.0 67.4 jit_solution(9968468995656176127)
XLA Ops:
  0.0 64.7 %shard_map.46 = f32[3,64,2048]{2,1,0:T(8,128)} custom-call(f32[16,64,2048]{2,1,0:T(8,128)} %field.1, s32[16]{0:T(128)} %rank.1, f32[2,3]{1,0:T(2,128)} %transfer.1, f32[3]{0:T(128)} %light_dir.1), custom_call_target="tpu_custom_call" | custom-call | tf_op jit(solution)/shard_map/pallas_call | solution.py:317
  64.7 2.7 %copy.6 = f32[3,64,2048]{2,1,0:T(8,128)} copy(f32[3,64,2048]{2,1,0:T(8,128)} %shard_map.46) | data formatting | bytes 3145728

commit v2 on v1

--- a/solution.py
+++ b/solution.py
@@ -11,7 +11,9 @@
 MESH = pl.DeviceIdType.MESH
 BACKGROUND = 0.25
 LOG2E = math.log2(math.e)
-LAG = 2
+LAG = 3
+GAP = 3
+DIRECT = 4
 PARTNERS = (
     (1, 2, 0), (1, 0, 0), (0, 2, 0), (0, 1, 0), (1, 1, 0), (0, 3, 0), (1, 3, 0),
     (1, 2, 1), (1, 0, 1), (0, 2, 1), (0, 1, 1), (1, 1, 1), (0, 3, 1), (1, 3, 1),
@@ -214,16 +216,26 @@
         ]
 
     def stage4(chunk):
-        return [gather_copy(chunk, 5, core * 8, 8, 0, 0, 1, ((core + 1) % 2) * 8)]
-
-    stages = (stage1, stage2, stage3, stage4)
+        return [gather_copy(chunk, 7, core * 8, 8, 0, 0, 1, ((core + 1) % 2) * 8)]
+
+    def spread(chunk):
+        return [
+            gather_copy(chunk, i, mine, 1, dy, dz, 0, column_block(dy, 4 - dz, 0))
+            for i, (dy, dz, dc) in enumerate(PARTNERS) if dc == 0
+        ]
+
+    order = list(range(1, chunks - 1)) + [0, chunks - 1]
+    stages = {
+        chunk: (stage1, stage2, stage3, stage4) if at < chunks - DIRECT else (spread, stage4)
+        for at, chunk in enumerate(order)
+    }
 
     def begin(stage, chunk):
-        for sent, _ in stages[stage](chunk):
+        for sent, _ in stages[chunk][stage](chunk):
             sent().start()
 
     def end(stage, chunk):
-        for _, got in stages[stage](chunk):
+        for _, got in stages[chunk][stage](chunk):
             got().wait_recv()
 
     def write(chunk):
@@ -246,8 +258,7 @@
         )
 
     has_up, has_down = row_part > 0, row_part < narrow - 1
-    order = list(range(1, chunks - 1)) + [0, chunks - 1]
-    last = chunks + LAG + 4
+    last = chunks + LAG + 4 * GAP
     for step in range(last):
         if step == 0:
             wait_load(0)
@@ -275,24 +286,25 @@
                 halo_down().start()
         if step < chunks:
             send_chunk(order[step])
-        for stage in range(4, -1, -1):
-            at = step - LAG - stage
-            if 0 <= at < chunks:
-                chunk = order[at]
-                if stage == 0:
-                    composite(chunk)
-                    begin(0, chunk)
-                else:
-                    end(stage - 1, chunk)
-                    if stage < 4:
-                        begin(stage, chunk)
-                    else:
-                        write(chunk).start()
+        for at in range(chunks):
+            chunk = order[at]
+            count = len(stages[chunk])
+            stage, rest = divmod(step - LAG - at, GAP)
+            if rest or not 0 <= stage <= count:
+                continue
+            if stage == 0:
+                composite(chunk)
+            else:
+                end(stage - 1, chunk)
+            if stage < count:
+                begin(stage, chunk)
+            else:
+                write(chunk).start()
 
     for chunk in range(chunks):
         all_of(chunk).wait_send()
-        for stage in range(4):
-            for sent, _ in stages[stage](chunk):
+        for stage in stages[chunk]:
+            for sent, _ in stage(chunk):
                 sent().wait_send()
         write(chunk).wait()
 
@@ -330,8 +342,8 @@
                 pltpu.SemaphoreType.DMA((2,)),
                 pltpu.SemaphoreType.DMA((chunks,)),
                 pltpu.SemaphoreType.DMA((chunks,)),
-                pltpu.SemaphoreType.DMA((chunks, 6)),
-                pltpu.SemaphoreType.DMA((chunks, 6)),
+                pltpu.SemaphoreType.DMA((chunks, 8)),
+                pltpu.SemaphoreType.DMA((chunks, 8)),
                 pltpu.SemaphoreType.DMA((chunks,)),
             ],
             compiler_params=pltpu.CompilerParams(collective_id=0, has_side_effects=True),

time: 67.5 us -> 52.8 us (0.78)
  Pallas kernels: 64.7 us -> 49.9 us
    pallas_call x1, Pallas kernels: 64.7 us -> 49.9 us  [body(): pl.pallas_call(functools.partial(kernel, (wide, narrow, rows, scale)), ou...]
where the time goes in v2:
time: 52.8 us; the launch traced here: 52.6 us
  Pallas kernels  49.9 us (95%)
  local copies, waits for them, and re-layouts  2.7 us (5%)
    pallas_call x1, Pallas kernels, body(): pl.pallas_call(functools.partial(kernel, (wide, narrow, rows, scale)), ou...  49.9 us
    unnamed x1, local copies, waits for them, and re-layouts  2.7 us

profile of v2, /device:TPU:1, one launch (start us, length us, event | category | flops | bytes accessed | tf_op | source)
XLA Modules:
  0.0 52.6 jit_solution(7872247755980565823)
XLA Ops:
  0.0 49.9 %shard_map.46 = f32[3,64,2048]{2,1,0:T(8,128)} custom-call(f32[16,64,2048]{2,1,0:T(8,128)} %field.1, s32[16]{0:T(128)} %rank.1, f32[2,3]{1,0:T(2,128)} %transfer.1, f32[3]{0:T(128)} %light_dir.1), custom_call_target="tpu_custom_call" | custom-call | tf_op jit(solution)/shard_map/pallas_call | solution.py:329
  49.9 2.7 %copy.6 = f32[3,64,2048]{2,1,0:T(8,128)} copy(f32[3,64,2048]{2,1,0:T(8,128)} %shard_map.46) | data formatting | bytes 3145728

commit v3 on v2

--- a/solution.py
+++ b/solution.py
@@ -15,8 +15,8 @@
 GAP = 3
 DIRECT = 4
 PARTNERS = (
-    (1, 2, 0), (1, 0, 0), (0, 2, 0), (0, 1, 0), (1, 1, 0), (0, 3, 0), (1, 3, 0),
-    (1, 2, 1), (1, 0, 1), (0, 2, 1), (0, 1, 1), (1, 1, 1), (0, 3, 1), (1, 3, 1),
+    (1, 2, 0), (1, 2, 1), (0, 2, 0), (0, 2, 1), (1, 1, 0), (1, 3, 1), (1, 3, 0), (1, 1, 1),
+    (1, 0, 0), (0, 1, 0), (0, 3, 1), (0, 3, 0), (0, 1, 1), (1, 0, 1),
     (0, 0, 1),
 )
 
@@ -221,7 +221,7 @@
     def spread(chunk):
         return [
             gather_copy(chunk, i, mine, 1, dy, dz, 0, column_block(dy, 4 - dz, 0))
-            for i, (dy, dz, dc) in enumerate(PARTNERS) if dc == 0
+            for i, (dy, dz) in enumerate([partner[:2] for partner in PARTNERS if partner[2] == 0])
         ]
 
     order = list(range(1, chunks - 1)) + [0, chunks - 1]
@@ -274,9 +274,12 @@
                     halo_up().wait_recv()
             compute(chunk)
         if step == 0:
+            pl.semaphore_wait(barrier, wide - 1 + has_up.astype(jnp.int32) + has_down.astype(jnp.int32))
+        if step < chunks:
+            send_chunk(order[step])
+        if step == 0:
             wait_load(1)
-            pl.semaphore_wait(barrier, wide - 1 + has_up.astype(jnp.int32) + has_down.astype(jnp.int32))
-
+        if step == 1:
             @pl.when(has_up)
             def _():
                 halo_up().start()
@@ -284,8 +287,7 @@
             @pl.when(has_down)
             def _():
                 halo_down().start()
-        if step < chunks:
-            send_chunk(order[step])
+
         for at in range(chunks):
             chunk = order[at]
             count = len(stages[chunk])

time: 52.8 us -> 52.5 us (level)
  no operation moved by 1% of the time
where the time goes in v3:
time: 52.5 us; the launch traced here: 52.4 us
  Pallas kernels  49.7 us (95%)
  local copies, waits for them, and re-layouts  2.7 us (5%)
    pallas_call x1, Pallas kernels, body(): pl.pallas_call(functools.partial(kernel, (wide, narrow, rows, scale)), ou...  49.7 us
    unnamed x1, local copies, waits for them, and re-layouts  2.7 us

profile of v3, /device:TPU:1, one launch (start us, length us, event | category | flops | bytes accessed | tf_op | source)
XLA Modules:
  0.0 52.4 jit_solution(18197423018090497390)
XLA Ops:
  0.0 49.7 %shard_map.46 = f32[3,64,2048]{2,1,0:T(8,128)} custom-call(f32[16,64,2048]{2,1,0:T(8,128)} %field.1, s32[16]{0:T(128)} %rank.1, f32[2,3]{1,0:T(2,128)} %transfer.1, f32[3]{0:T(128)} %light_dir.1), custom_call_target="tpu_custom_call" | custom-call | tf_op jit(solution)/shard_map/pallas_call | solution.py:331
  49.7 2.7 %copy.6 = f32[3,64,2048]{2,1,0:T(8,128)} copy(f32[3,64,2048]{2,1,0:T(8,128)} %shard_map.46) | data formatting | bytes 3145728
